TPU v7x, 32 devices: a whole 2x2x4 slice. The times are simulated.
32 devices in a mesh: groups: 2 (over y), seq: 16 (over z, x, core).
Axes of the slice: x: 2, y: 2, z: 4, core: 2. Of those that a mesh axis runs over, the one named last changes fastest.
Arguments:
- queries: bfloat16 [4, 128, 128, 128], P('groups', 'seq'), parts along dimension 0, may hold values from -64 to 64
- new_k: bfloat16 [4, 128, 8, 128], P('groups', 'seq'), parts along dimension 0, may hold values from -15 to 15
- new_v: bfloat16 [4, 128, 8, 128], P('groups', 'seq'), parts along dimension 0, may hold values from -6 to 6
- cache_k: bfloat16 [4, 8192, 8, 128], P('groups', 'seq'), parts along dimension 0, may hold values from -12 to 12
- cache_v: bfloat16 [4, 8192, 8, 128], P('groups', 'seq'), parts along dimension 0, may hold values from -6 to 6
- cache_len: int32 [4], P('groups'), parts along dimension 0, may hold values from 2048 to 8192
Outputs:
- attended: bfloat16 [4, 128, 128, 128], P('groups', 'seq'), parts along dimension 0
There are 2 independent parts, one for each index of `groups`. A program takes and returns all parts, laid end to end along the dimension named above; each array names one. Nothing has to cross between parts.
Inputs may be any that keep to these rules, and one draw needn't show every extreme that they name: The first cache_len[r] of the 8192 cache slots of request r hold keys and values; the rest are to be ignored.
All inputs are finite; a program needn't handle non-finite values.
Results may differ from a plain program's by a relative error of at most 0.004.
Values may be sent and summed in bfloat16 or wider, within the bound.
No kernel may reach another device: no remote copies, remote signals or barrier semaphores. Data moves between devices by JAX's collectives and lax.ppermute only.
A program may use at most 128 MiB of HBM per device.

v0:
```python
import functools
import math

import jax
import jax.numpy as jnp
from jax import lax
from jax.experimental import pallas as pl
from jax.experimental.pallas import tpu as pltpu
from jax.sharding import PartitionSpec as P


NEG = -1e30
STAT_ROWS = 8
SMALL_VMEM = 12 * 2**20
LARGE_VMEM = 56 * 2**20


VMEM_SPEC = pl.BlockSpec(memory_space=pltpu.VMEM)
HBM_SPEC = pl.BlockSpec(memory_space=pltpu.HBM)
SMEM_SPEC = pl.BlockSpec(memory_space=pltpu.SMEM)


def attend_kernel(*refs, order, blocks, tile, group_size, row_start, with_fresh, with_state, final):
    refs = list(refs)
    length_ref, place_ref, q_hbm = refs.pop(0), refs.pop(0), refs.pop(0)
    kv_refs = [refs.pop(0) for _ in order]
    if with_fresh:
        fk_ref, fv_ref = refs.pop(0), refs.pop(0)
    if with_state:
        acc_in, top_in = refs.pop(0), refs.pop(0)
    if final:
        out_hbm = refs.pop(0)
        out_ref, out_sem = refs.pop(), refs.pop()
    else:
        acc_out, top_out = refs.pop(0), refs.pop(0)
    q_ref, keys, loaded, vals, bias, s0, s1, m0, m1, in_sems, q_sem = refs
    per_source, dim = q_ref.shape[1:]
    block_slots = kv_refs[0].shape[1]
    chunk = bias.shape[0]
    slots = len(order) * block_slots
    chunks = slots // chunk
    fresh = fk_ref.shape[0] if with_fresh else 0
    rows = q_ref.shape[0] * per_source
    tiles = rows // tile
    span = tile // per_source
    ones = vals.shape[0] - dim
    scale = math.log2(math.e) / math.sqrt(dim)
    own, device_block = place_ref[0], place_ref[1]
    valid = jnp.clip(length_ref[0] - device_block * blocks * block_slots, 0, blocks * block_slots)
    fresh_shift = jnp.where(device_block == q_ref.shape[0] // blocks - 1, 0, -rows)

    held = sorted({k // 2 for k in order})
    absent = [c for c in range(blocks // 2) if c not in held]

    def rank_of(index):
        rank = index
        for c in absent:
            rank = rank - jnp.where((own // 2) ^ c < index, 1, 0)
        return rank

    value_copies = []
    copies = []
    for i, k in enumerate(order):
        first = rank_of((own // 2) ^ (k // 2)) * chunk + ((own % 2) ^ (k % 2)) * block_slots
        at = pl.ds(pl.multiple_of(first, block_slots), block_slots)
        value_copies.append(pltpu.make_async_copy(kv_refs[i].at[1], loaded.at[at, :], in_sems.at[i, 1]))
        copies.append(pltpu.make_async_copy(kv_refs[i].at[0], keys.at[at, :], in_sems.at[i, 0]))
    copies.append(pltpu.make_async_copy(q_hbm.at[:, row_start : row_start + per_source, :], q_ref, q_sem))
    for copy in value_copies + copies:
        copy.start()

    filled = jnp.int32(0)
    last_valid = jnp.int32(0)
    for c in held:
        left = valid - ((own // 2) ^ c) * chunk
        filled = filled + jnp.where(left > 0, 1, 0)
        last_valid = jnp.where((left > 0) & (left < chunk), left, last_valid)
    last_valid = jnp.where(last_valid == 0, chunk, last_valid)

    vals[dim:, :] = jnp.ones((ones, slots + fresh), jnp.bfloat16)
    if with_fresh:
        vals[:dim, slots:] = jnp.transpose(fv_ref[...])
    bias[...] = jnp.where(lax.broadcasted_iota(jnp.int32, bias.shape, 0) < last_valid, 0.0, NEG)
    for copy in copies + value_copies:
        copy.wait()

    def turn_values(count):
        for first in range(0, count * chunk, block_slots):
            vals[:dim, first : first + block_slots] = jnp.transpose(loaded[first : first + block_slots, :])

    def fold_max(scores, best):
        part = jnp.max(scores.reshape(-1, 8, tile), axis=0)
        return part if best is None else jnp.maximum(best, part)

    def score_chunk(t, j, count, s_ref, best):
        q = q_ref[pl.ds(t * span, span)].reshape(tile, dim)
        at = slice(j * chunk, (j + 1) * chunk) if j < count else slice(slots, slots + fresh)
        left_side = keys[at, :] if j < count else fk_ref[...]
        scores = lax.dot_general(left_side, q, (((1,), (1,)), ((), ())), preferred_element_type=jnp.float32)
        if j == count - 1:
            mask = bias[...]
            scores = scores + jnp.concatenate([mask] * (tile // mask.shape[1]), axis=1)
        elif j == count:
            token = (t * tile + lax.broadcasted_iota(jnp.int32, (1, tile), 1)) // group_size
            unit = lax.broadcasted_iota(jnp.int32, (fresh, 1), 0)
            scores = jnp.where(unit <= token + fresh_shift, scores, NEG)
        s_ref[at, :] = scores
        return fold_max(scores, best)

    def value_chunk(j, count, s_ref, top, acc):
        at = slice(j * chunk, (j + 1) * chunk) if j < count else slice(slots, slots + fresh)
        weights = jnp.exp2((s_ref[at, :] - top) * scale).astype(jnp.bfloat16)
        part = jnp.dot(vals[:, at], weights, preferred_element_type=jnp.float32)
        return part if acc is None else acc + part

    def finish(t, top, acc):
        total = acc[dim : dim + 1, :]
        out = (acc[:dim, :] * (1.0 / total)).astype(jnp.bfloat16)
        level = top * scale + jnp.log2(total)
        high = level.astype(jnp.bfloat16).astype(jnp.float32)
        mid = (level - high).astype(jnp.bfloat16).astype(jnp.float32)
        low = level - high - mid
        which = lax.broadcasted_iota(jnp.int32, (STAT_ROWS, tile), 0)
        stats = jnp.where(which == 0, high, jnp.where(which == 1, mid, low)).astype(jnp.bfloat16)
        for first in range(0, tile, dim):
            flat = jnp.transpose(out[:, first : first + dim])
            width = min(per_source, dim)
            for part in range(dim // width):
                source = t * span + (first + part * width) // per_source
                inside = (first + part * width) % per_source
                out_ref[source, inside : inside + width, :] = flat[part * width : (part + 1) * width, :]
                out_ref[source, per_source:, inside : inside + width] = stats[
                    :, first + part * width : first + (part + 1) * width
                ]

    def stage(t_next, s_next, m_next, t_now, s_now, m_now, count):
        pieces = count + (1 if with_fresh else 0)
        best = None
        acc = None
        if t_now is not None:
            at = pl.ds(pl.multiple_of(t_now * tile, tile), tile)
            top = jnp.max(m_now[...], axis=0, keepdims=True) if pieces else None
            if with_state:
                before = top_in[:, at][:1]
                top = before if top is None else jnp.maximum(top, before)
                acc = acc_in[:, at] * jnp.exp2((before - top) * scale)
        for j in range(pieces):
            if t_next is not None:
                best = score_chunk(t_next, j, count, s_next, best)
            if t_now is not None:
                acc = value_chunk(j, count, s_now, top, acc)
        if t_next is not None and pieces:
            m_next[...] = best
        if t_now is not None:
            if final:
                finish(t_now, top, acc)
            else:
                acc_out[:, at] = acc
                top_out[:, at] = jnp.broadcast_to(top, (8, tile))

    for count in range(chunks + 1):

        @pl.when(filled == count)
        def _(count=count):
            stage(0, s0, m0, None, None, None, count)
            turn_values(count)

            def pair(i, carry):
                stage(2 * i + 1, s1, m1, 2 * i, s0, m0, count)
                stage(2 * i + 2, s0, m0, 2 * i + 1, s1, m1, count)
                return carry

            lax.fori_loop(0, tiles // 2 - 1, pair, 0)
            last = jnp.int32(tiles - 1)
            stage(last, s1, m1, last - 1, s0, m0, count)
            stage(None, None, None, last, s1, m1, count)

    if final:
        result = pltpu.make_async_copy(out_ref, out_hbm, out_sem)
        result.start()
        result.wait()


def attend(length, place, head_q, kv_blocks, order, fresh, state, final, row_start, row_count, group_size):
    sources, _, dim = head_q.shape
    slots = len(order) * kv_blocks[0].shape[1]
    rows = sources * row_count
    units = 0 if fresh is None else fresh[0].shape[0]
    tile = min(256, rows // 2)
    chunk = 2 * kv_blocks[0].shape[1]
    depth = dim + 16
    operands = [length, place, head_q] + [kv_blocks[k] for k in order]
    in_specs = [SMEM_SPEC] * 2 + [HBM_SPEC] * (1 + len(order))
    scratch = [
        pltpu.VMEM((sources, row_count, dim), jnp.bfloat16),
        pltpu.VMEM((slots, dim), jnp.bfloat16),
        pltpu.VMEM((slots, dim), jnp.bfloat16),
        pltpu.VMEM((depth, slots + units), jnp.bfloat16),
        pltpu.VMEM((chunk, min(dim, tile)), jnp.float32),
        pltpu.VMEM((slots + units, tile), jnp.float32),
        pltpu.VMEM((slots + units, tile), jnp.float32),
        pltpu.VMEM((8, tile), jnp.float32),
        pltpu.VMEM((8, tile), jnp.float32),
        pltpu.SemaphoreType.DMA((len(order), 2)),
        pltpu.SemaphoreType.DMA,
    ]
    if fresh is not None:
        operands += list(fresh)
        in_specs += [VMEM_SPEC] * 2
    if state is not None:
        operands += list(state)
        in_specs += [VMEM_SPEC] * 2
    if final:
        out_shape = jax.ShapeDtypeStruct((sources, row_count + STAT_ROWS, dim), jnp.bfloat16)
        out_specs = HBM_SPEC
        scratch += [pltpu.SemaphoreType.DMA, pltpu.VMEM(out_shape.shape, jnp.bfloat16)]
    else:
        out_shape = [
            jax.ShapeDtypeStruct((depth, rows), jnp.float32),
            jax.ShapeDtypeStruct((8, rows), jnp.float32),
        ]
        out_specs = [VMEM_SPEC] * 2
    grant = 8 * tile * (slots + units) + 8 * slots * dim + 12 * rows * dim + SMALL_VMEM
    return pl.pallas_call(
        functools.partial(
            attend_kernel,
            order=order,
            blocks=len(kv_blocks),
            tile=tile,
            group_size=group_size,
            row_start=row_start,
            with_fresh=fresh is not None,
            with_state=state is not None,
            final=final,
        ),
        in_specs=in_specs,
        out_specs=out_specs,
        scratch_shapes=scratch,
        out_shape=out_shape,
        compiler_params=pltpu.CompilerParams(vmem_limit_bytes=grant),
        cost_estimate=pl.CostEstimate(
            flops=4 * rows * slots * dim,
            bytes_accessed=4 * slots * dim + 4 * rows * dim,
            transcendentals=rows * slots,
        ),
    )(*operands)


def merge_kernel(part_ref, *refs, group_size):
    out_ref = refs[-1]
    spread, heads, _, dim = part_ref.shape
    local_rows = out_ref.shape[1]
    per_source = local_rows * group_size
    levels = []
    for b in range(spread):
        stats = [
            part_ref[b, h, per_source : per_source + STAT_ROWS, :].astype(jnp.float32) for h in range(heads)
        ]
        levels.append(jnp.concatenate([x[0:1] + x[1:2] + x[2:3] for x in stats], axis=0))
    top = functools.reduce(jnp.maximum, levels)
    weights = [jnp.exp2(level - top) for level in levels]
    total = functools.reduce(jnp.add, weights)
    weights = [jnp.transpose(w / total) for w in weights]
    for h in range(heads):
        mixed = functools.reduce(
            jnp.add,
            [
                w[:per_source, h : h + 1] * part_ref[b, h, :per_source, :].astype(jnp.float32)
                for b, w in enumerate(weights)
            ],
        ).astype(jnp.bfloat16)
        out_ref[0, :, h * group_size : (h + 1) * group_size, :] = mixed.reshape(local_rows, group_size, dim)


def merge(parts, request, requests, local_rows, group_size, earlier):
    heads, dim = parts.shape[1], parts.shape[3]
    rest = [] if earlier is None else [earlier]
    return pl.pallas_call(
        functools.partial(merge_kernel, group_size=group_size),
        grid=(1,),
        in_specs=[pl.BlockSpec(parts.shape, lambda i: (0, 0, 0, 0))]
        + [pl.BlockSpec(memory_space=pl.ANY) for _ in rest],
        out_specs=pl.BlockSpec((1, local_rows, heads * group_size, dim), lambda i: (request, 0, 0, 0)),
        out_shape=jax.ShapeDtypeStruct((requests, local_rows, heads * group_size, dim), jnp.bfloat16),
        input_output_aliases={1: 0} if rest else {},
        compiler_params=pltpu.CompilerParams(vmem_limit_bytes=SMALL_VMEM),
    )(parts, *rest)


def pack_kernel(q_ref, k_ref, v_ref, out_ref):
    requests, local_rows, heads, dim = q_ref.shape
    kv_heads = k_ref.shape[2]
    group_size = heads // kv_heads
    rows = requests * local_rows * group_size
    units = requests * local_rows
    fresh = [jnp.swapaxes(ref[...].reshape(units, kv_heads, dim), 0, 1) for ref in (k_ref, v_ref)]
    for d in range(out_ref.shape[0]):
        head = d % kv_heads
        out_ref[d, :rows, :] = q_ref[:, :, head * group_size : (head + 1) * group_size, :].reshape(rows, dim)
        out_ref[d, rows : rows + units, :] = fresh[0][head]
        out_ref[d, rows + units :, :] = fresh[1][head]


def pack(queries, new_k, new_v, devices):
    requests, local_rows, heads, dim = queries.shape
    kv_heads = new_k.shape[2]
    rows = requests * local_rows * (heads // kv_heads + 2)
    return pl.pallas_call(
        pack_kernel,
        in_specs=[VMEM_SPEC] * 3,
        out_specs=VMEM_SPEC,
        out_shape=jax.ShapeDtypeStruct((devices, rows, dim), jnp.bfloat16),
        compiler_params=pltpu.CompilerParams(vmem_limit_bytes=SMALL_VMEM),
    )(queries, new_k, new_v)


def split_kernel(own_ref, k_hbm, v_hbm, *refs, request):
    loaded, held, sems = refs[-3:]
    copies = [
        pltpu.make_async_copy(hbm.at[request], loaded.at[i], sems.at[i]) for i, hbm in enumerate((k_hbm, v_hbm))
    ]
    for copy in copies:
        copy.start()
    for i, copy in enumerate(copies):
        copy.wait()
        held[:, i] = jnp.swapaxes(loaded[i], 0, 1)
    for k, out_ref in enumerate(refs[:-3]):
        out_ref[...] = held[own_ref[0] ^ k]


def split_heads(own, cache_k, cache_v, request, grant):
    _, slots, kv_heads, dim = cache_k.shape
    return pl.pallas_call(
        functools.partial(split_kernel, request=request),
        in_specs=[SMEM_SPEC, HBM_SPEC, HBM_SPEC],
        out_specs=[VMEM_SPEC] * kv_heads,
        out_shape=[jax.ShapeDtypeStruct((2, slots, dim), jnp.bfloat16)] * kv_heads,
        scratch_shapes=[
            pltpu.VMEM((2, slots, kv_heads, dim), jnp.bfloat16),
            pltpu.VMEM((kv_heads, 2, slots, dim), jnp.bfloat16),
            pltpu.SemaphoreType.DMA((2,)),
        ],
        compiler_params=pltpu.CompilerParams(vmem_limit_bytes=grant),
    )(own, cache_k, cache_v)


def attention(queries, new_k, new_v, cache_k, cache_v, cache_len):
    requests, local_rows, heads, head_dim = queries.shape
    kv_heads = cache_k.shape[2]
    group_size = heads // kv_heads
    devices_seq = lax.axis_size("seq")
    seq_index = lax.axis_index("seq")
    spread = devices_seq // kv_heads
    block = seq_index // kv_heads
    own = (seq_index % kv_heads).astype(jnp.int32)
    per_source = local_rows * group_size

    head_q = lax.all_to_all(pack(queries, new_k, new_v, devices_seq), "seq", split_axis=0, concat_axis=0, tiled=True)
    head_fresh = head_q[:, requests * per_source :, :].reshape(
        devices_seq, 2, requests, local_rows, head_dim
    )
    head_fresh = jnp.transpose(head_fresh, (1, 2, 0, 3, 4)).reshape(
        2, requests, devices_seq * local_rows, head_dim
    )

    kv_blocks = []
    for r in range(requests):
        parts = split_heads(own[None], cache_k, cache_v, r, LARGE_VMEM if r == 0 else 2 * SMALL_VMEM)
        moved = [parts[0]]
        for k in range(1, kv_heads):
            moved.append(lax.ppermute(parts[k], "seq", [(i, i ^ k) for i in range(devices_seq)]))
        kv_blocks.append(moved)

    place = jnp.stack([own, block]).astype(jnp.int32)
    out = None
    for r in range(requests):
        rows = (r * per_source, per_source, group_size)
        common = (cache_len[r : r + 1], place, head_q, kv_blocks[r])
        fresh_r = (head_fresh[0, r], head_fresh[1, r])
        first = kv_heads - 2
        state = attend(*common, tuple(range(first)), fresh_r, None, False, *rows)
        part = attend(*common, tuple(range(first, kv_heads)), None, state, True, *rows)
        part = lax.all_to_all(part, "seq", split_axis=0, concat_axis=0, tiled=True)
        part = part.reshape(spread, kv_heads, per_source + STAT_ROWS, head_dim)
        out = merge(part, r, requests, local_rows, group_size, out)
    return out


def solution(mesh):
    in_specs = (
        P("groups", "seq", None, None),
        P("groups", "seq", None, None),
        P("groups", "seq", None, None),
        P("groups", "seq", None, None),
        P("groups", "seq", None, None),
        P("groups"),
    )
    out_specs = P("groups", "seq", None, None)
    return jax.shard_map(attention, mesh=mesh, in_specs=in_specs, out_specs=out_specs, check_vma=False)
```

profile of v0, /device:TPU:0, one launch (start us, length us, event | category | flops | bytes accessed | tf_op | source)
XLA Modules:
  0.0 126.9 jit_solution(5773595333868504662)
XLA Ops:
  3.7 7.4 %all-to-all-start = ((bf16[16,288,128]{2,1,0:T(8,128)(2,1)}), bf16[16,288,128]{2,1,0:T(8,128)(2,1)S(1)}, u32[]{:S(2)}, u32[]{:S(2)}) async-start(bf16[16,288,128]{2,1,0:T(8,128)(2,1)} %shard_map.64), calls=%async_computation | async-start | bytes 2359296 | tf_op jit(solution)/shard_map/all_to_all | solution.py:358
  11.1 3.3 %shard_map.68 = (bf16[2,512,128]{2,1,0:T(8,128)(2,1)}, bf16[2,512,128]{2,1,0:T(8,128)(2,1)}, bf16[2,512,128]{2,1,0:T(8,128)(2,1)}, bf16[2,512,128]{2,1,0:T(8,128...) custom-call(s32[1]{0:T(128)} %bitcast.own_ref, ...), custom_call_target="tpu_custom_call" | custom-call | tf_op jit(solution)/shard_map/pallas_call | solution.py:333
  14.9 1.6 %collective-permute-start.10 = (bf16[2,512,128]{2,1,0:T(8,128)(2,1)}, bf16[2,512,128]{2,1,0:T(8,128)(2,1)S(1)}, u32[]{:S(2)}, u32[]{:S(2)}) collective-permute-start(bf16[2,512,128]{2,1,0:T(8,128)(2,1)} %get-tuple-element.39), channel_id=1, source_target_pairs={{0,2},{1,3},{2,0},{3,1},{4,6},{5,7},{6,4},{7,5},{8,10},{9,11},{10,... | collective-permute-start | bytes 786440 | tf_op jit(solution)/shard_map/ppermute | solution.py:371
  16.5 1.7 %collective-permute-start.12 = (bf16[2,512,128]{2,1,0:T(8,128)(2,1)}, bf16[2,512,128]{2,1,0:T(8,128)(2,1)S(1)}, u32[]{:S(2)}, u32[]{:S(2)}) collective-permute-start(bf16[2,512,128]{2,1,0:T(8,128)(2,1)} %get-tuple-element.41), channel_id=1, source_target_pairs={{0,4},{1,5},{2,6},{3,7},{4,0},{5,1},{6,2},{7,3},{8,12},{9,13},{10,... | collective-permute-start | bytes 786440 | tf_op jit(solution)/shard_map/ppermute | solution.py:371
  19.1 17.5 %all-to-all-done.refs_2_ = bf16[16,288,128]{2,1,0:T(8,128)(2,1)S(1)} async-done(((bf16[16,288,128]{2,1,0:T(8,128)(2,1)}), bf16[16,288,128]{2,1,0:T(8,128)(2,1)S(1)}, u32[]{:S(2)}, u32[]{:S(2)}) %all-to-all-start) | async-done | bytes 1179680 | tf_op jit(solution)/shard_map/all_to_all | solution.py:358
  36.7 4.9 %collective-permute-start.7 = (bf16[2,512,128]{2,1,0:T(8,128)(2,1)}, bf16[2,512,128]{2,1,0:T(8,128)(2,1)S(1)}, u32[]{:S(2)}, u32[]{:S(2)}) collective-permute-start(bf16[2,512,128]{2,1,0:T(8,128)(2,1)} %get-tuple-element.35), channel_id=1, source_target_pairs={{0,6},{1,7},{2,4},{3,5},{4,2},{5,3},{6,0},{7,1},{8,14},{9,15},{10,... | collective-permute-start | bytes 786440 | tf_op jit(solution)/shard_map/ppermute | solution.py:371
  41.9 1.9 %collective-permute-done.13.refs_8_ = bf16[2,512,128]{2,1,0:T(8,128)(2,1)S(1)} collective-permute-done((bf16[2,512,128]{2,1,0:T(8,128)(2,1)}, bf16[2,512,128]{2,1,0:T(8,128)(2,1)S(1)}, u32[]{:S(2)}, u32[]{:S(2)}) %collective-permute-start.13) | collective-permute-done | bytes 262176 | tf_op jit(solution)/shard_map/ppermute | solution.py:371
  44.7 10.4 %shard_map.69 = (f32[144,2048]{1,0:T(8,128)S(1)}, f32[8,2048]{1,0:T(8,128)S(1)}) custom-call(s32[1]{0:T(128)} %get-tuple-element.49.refs_0_, s32[2]{0:T(128)S(1)} %pad_add_fusion.refs_1_, bf16[16,288,128]{2,1,0:T(8,128)(2,1)S(1)} %all-to-all-done.refs_2_, bf16[2,512,128]{2,1,0:T(8,128)(2,1)S(1)} %copy-done.8, ...), custom_call_target="tpu_custom_call" | custom-call | flops 3221225472 | bytes 2621440 | tf_op jit(solution)/shard_map/pallas_call | solution.py:224
  56.0 6.1 %shard_map.70 = bf16[16,136,128]{2,1,0:T(8,128)(2,1)S(1)} custom-call(s32[1]{0:T(128)} %get-tuple-element.49.refs_0_, s32[2]{0:T(128)S(1)} %pad_add_fusion.refs_1_, bf16[16,288,128]{2,1,0:T(8,128)(2,1)S(1)} %all-to-all-done.refs_2_, bf16[2,512,128]{2,1,0:T(8,128)(2,1)S(1)} %collective-permute-done.7.refs_3_, ...), custom_call_target="tpu_custom_call" | custom-call | flops 1073741824 | bytes 1572864 | tf_op jit(solution)/shard_map/pallas_call | solution.py:224
  62.9 4.1 %all-to-all-start.2 = ((bf16[16,136,128]{2,1,0:T(8,128)(2,1)}), bf16[16,136,128]{2,1,0:T(8,128)(2,1)S(1)}, u32[]{:S(2)}, u32[]{:S(2)}) async-start(bf16[16,136,128]{2,1,0:T(8,128)(2,1)} %copy-done.4), calls=%async_computation.2 | async-start | bytes 1114112 | tf_op jit(solution)/shard_map/all_to_all | solution.py:383
  67.0 1.6 %copy-done.1 = bf16[2,512,8,128]{3,2,1,0:T(8,128)(2,1)S(1)} copy-done((bf16[2,512,8,128]{3,2,1,0:T(8,128)(2,1)S(1)}, bf16[2,512,8,128]{3,2,1,0:T(8,128)(2,1)}, u32[]{:S(2)}) %copy-start.1) | copy-done | bytes 2097176
  70.1 1.6 %collective-permute-start.3 = (bf16[2,512,128]{2,1,0:T(8,128)(2,1)S(1)}, bf16[2,512,128]{2,1,0:T(8,128)(2,1)S(1)}, u32[]{:S(2)}, u32[]{:S(2)}) collective-permute-start(bf16[2,512,128]{2,1,0:T(8,128)(2,1)S(1)} %get-tuple-element.29), channel_id=1, source_target_pairs={{0,2},{1,3},{2,0},{3,1},{4,6},{5,7},{6,4},{7,5},{8,10},{9,11},{10,... | collective-permute-start | bytes 786440 | tf_op jit(solution)/shard_map/ppermute | solution.py:371
  71.7 1.7 %collective-permute-start.5 = (bf16[2,512,128]{2,1,0:T(8,128)(2,1)S(1)}, bf16[2,512,128]{2,1,0:T(8,128)(2,1)S(1)}, u32[]{:S(2)}, u32[]{:S(2)}) collective-permute-start(bf16[2,512,128]{2,1,0:T(8,128)(2,1)S(1)} %get-tuple-element.31), channel_id=1, source_target_pairs={{0,4},{1,5},{2,6},{3,7},{4,0},{5,1},{6,2},{7,3},{8,12},{9,13},{10,... | collective-permute-start | bytes 786440 | tf_op jit(solution)/shard_map/ppermute | solution.py:371
  73.6 2.5 %collective-permute-start = (bf16[2,512,128]{2,1,0:T(8,128)(2,1)S(1)}, bf16[2,512,128]{2,1,0:T(8,128)(2,1)S(1)}, u32[]{:S(2)}, u32[]{:S(2)}) collective-permute-start(bf16[2,512,128]{2,1,0:T(8,128)(2,1)S(1)} %get-tuple-element.25), channel_id=1, source_target_pairs={{0,6},{1,7},{2,4},{3,5},{4,2},{5,3},{6,0},{7,1},{8,14},{9,15},{10,... | collective-permute-start | bytes 786440 | tf_op jit(solution)/shard_map/ppermute | solution.py:371
  76.1 6.1 %collective-permute-done.3.refs_5_ = bf16[2,512,128]{2,1,0:T(8,128)(2,1)S(1)} collective-permute-done((bf16[2,512,128]{2,1,0:T(8,128)(2,1)S(1)}, bf16[2,512,128]{2,1,0:T(8,128)(2,1)S(1)}, u32[]{:S(2)}, u32[]{:S(2)}) %collective-permute-start.3) | collective-permute-done | bytes 262176 | tf_op jit(solution)/shard_map/ppermute | solution.py:371
  82.2 1.4 %collective-permute-start.1 = (bf16[2,512,128]{2,1,0:T(8,128)(2,1)S(1)}, bf16[2,512,128]{2,1,0:T(8,128)(2,1)S(1)}, u32[]{:S(2)}, u32[]{:S(2)}) collective-permute-start(bf16[2,512,128]{2,1,0:T(8,128)(2,1)S(1)} %get-tuple-element.26), channel_id=1, source_target_pairs={{0,7},{1,6},{2,5},{3,4},{4,3},{5,2},{6,1},{7,0},{8,15},{9,14},{10,... | collective-permute-start | bytes 786440 | tf_op jit(solution)/shard_map/ppermute | solution.py:371
  83.6 3.4 %collective-permute-done.4.refs_6_ = bf16[2,512,128]{2,1,0:T(8,128)(2,1)S(1)} collective-permute-done((bf16[2,512,128]{2,1,0:T(8,128)(2,1)S(1)}, bf16[2,512,128]{2,1,0:T(8,128)(2,1)S(1)}, u32[]{:S(2)}, u32[]{:S(2)}) %collective-permute-start.4) | collective-permute-done | bytes 262176 | tf_op jit(solution)/shard_map/ppermute | solution.py:371
  87.0 2.7 %collective-permute-done.6.refs_8_ = bf16[2,512,128]{2,1,0:T(8,128)(2,1)S(1)} collective-permute-done((bf16[2,512,128]{2,1,0:T(8,128)(2,1)S(1)}, bf16[2,512,128]{2,1,0:T(8,128)(2,1)S(1)}, u32[]{:S(2)}, u32[]{:S(2)}) %collective-permute-start.6) | collective-permute-done | bytes 262176 | tf_op jit(solution)/shard_map/ppermute | solution.py:371
  89.7 10.4 %shard_map.66 = (f32[144,2048]{1,0:T(8,128)S(1)}, f32[8,2048]{1,0:T(8,128)S(1)}) custom-call(s32[1]{0:T(128)} %get-tuple-element.50.refs_0_, s32[2]{0:T(128)S(1)} %pad_add_fusion.refs_1_, bf16[16,288,128]{2,1,0:T(8,128)(2,1)S(1)} %copy-done.3, bf16[2,512,128]{2,1,0:T(8,128)(2,1)S(1)} %get-tuple-element.27.refs_3_, ...), custom_call_target="tpu_custom_call" | custom-call | flops 3221225472 | bytes 2621440 | tf_op jit(solution)/shard_map/pallas_call | solution.py:224
  100.1 2.1 %collective-permute-done.1.refs_4_ = bf16[2,512,128]{2,1,0:T(8,128)(2,1)S(1)} collective-permute-done((bf16[2,512,128]{2,1,0:T(8,128)(2,1)S(1)}, bf16[2,512,128]{2,1,0:T(8,128)(2,1)S(1)}, u32[]{:S(2)}, u32[]{:S(2)}) %collective-permute-start.1) | collective-permute-done | bytes 262176 | tf_op jit(solution)/shard_map/ppermute | solution.py:371
  102.2 3.4 %shard_map.67 = bf16[16,136,128]{2,1,0:T(8,128)(2,1)} custom-call(s32[1]{0:T(128)} %get-tuple-element.50.refs_0_, s32[2]{0:T(128)S(1)} %pad_add_fusion.refs_1_, bf16[16,288,128]{2,1,0:T(8,128)(2,1)S(1)} %copy-done.3, bf16[2,512,128]{2,1,0:T(8,128)(2,1)S(1)} %collective-permute-done.refs_3_, bf16[2,512,128]{2,1,0:T(8,128)(2,1)S(1)} %collective-permute-done.1.refs_4_, ...), custom_call_target="tpu_custom_call" | custom-call | flops 1073741824 | bytes 1572864 | tf_op jit(solution)/shard_map/pallas_call | solution.py:224
  105.7 5.1 %all-to-all-start.1 = ((bf16[16,136,128]{2,1,0:T(8,128)(2,1)}), bf16[16,136,128]{2,1,0:T(8,128)(2,1)S(1)}, u32[]{:S(2)}, u32[]{:S(2)}) async-start(bf16[16,136,128]{2,1,0:T(8,128)(2,1)} %shard_map.67), calls=%async_computation.1 | async-start | bytes 1114112 | tf_op jit(solution)/shard_map/all_to_all | solution.py:383
  110.9 1.3 shard_map.71.refs_0_
  112.1 13.5 %all-to-all-done.1 = bf16[16,136,128]{2,1,0:T(8,128)(2,1)S(1)} async-done(((bf16[16,136,128]{2,1,0:T(8,128)(2,1)}), bf16[16,136,128]{2,1,0:T(8,128)(2,1)S(1)}, u32[]{:S(2)}, u32[]{:S(2)}) %all-to-all-start.1) | async-done | bytes 557088 | tf_op jit(solution)/shard_map/all_to_all | solution.py:383
  (44 shorter events, 10.9 us)
Async XLA Ops:
  0.0 1.0 copy-start.5
  3.7 32.9 %all-to-all-start = ((bf16[16,288,128]{2,1,0:T(8,128)(2,1)}), bf16[16,288,128]{2,1,0:T(8,128)(2,1)S(1)}, u32[]{:S(2)}, u32[]{:S(2)}) async-start(bf16[16,288,128]{2,1,0:T(8,128)(2,1)} %shard_map.64), calls=%async_computation | async-start | bytes 2359296 | tf_op jit(solution)/shard_map/all_to_all | solution.py:358
  11.1 7.3 %copy-start.9 = (s32[2]{0:T(128)S(1)}, s32[2]{0:T(128)}, u32[]{:S(2)}) copy-start(s32[2]{0:T(128)} %param.11) | copy-start | bytes 28
  14.4 22.3 %collective-permute-start.9 = (bf16[2,512,128]{2,1,0:T(8,128)(2,1)}, bf16[2,512,128]{2,1,0:T(8,128)(2,1)S(1)}, u32[]{:S(2)}, u32[]{:S(2)}) collective-permute-start(bf16[2,512,128]{2,1,0:T(8,128)(2,1)} %get-tuple-element.38), channel_id=1, source_target_pairs={{0,1},{1,0},{2,3},{3,2},{4,5},{5,4},{6,7},{7,6},{8,9},{9,8},{10,11... | collective-permute-start | bytes 786440 | tf_op jit(solution)/shard_map/ppermute | solution.py:371
  14.9 26.7 %collective-permute-start.10 = (bf16[2,512,128]{2,1,0:T(8,128)(2,1)}, bf16[2,512,128]{2,1,0:T(8,128)(2,1)S(1)}, u32[]{:S(2)}, u32[]{:S(2)}) collective-permute-start(bf16[2,512,128]{2,1,0:T(8,128)(2,1)} %get-tuple-element.39), channel_id=1, source_target_pairs={{0,2},{1,3},{2,0},{3,1},{4,6},{5,7},{6,4},{7,5},{8,10},{9,11},{10,... | collective-permute-start | bytes 786440 | tf_op jit(solution)/shard_map/ppermute | solution.py:371
  16.5 25.4 %collective-permute-start.11 = (bf16[2,512,128]{2,1,0:T(8,128)(2,1)}, bf16[2,512,128]{2,1,0:T(8,128)(2,1)S(1)}, u32[]{:S(2)}, u32[]{:S(2)}) collective-permute-start(bf16[2,512,128]{2,1,0:T(8,128)(2,1)} %get-tuple-element.40), channel_id=1, source_target_pairs={{0,3},{1,2},{2,1},{3,0},{4,7},{5,6},{6,5},{7,4},{8,11},{9,10},{10,... | collective-permute-start | bytes 786440 | tf_op jit(solution)/shard_map/ppermute | solution.py:371
  16.5 25.4 %collective-permute-start.12 = (bf16[2,512,128]{2,1,0:T(8,128)(2,1)}, bf16[2,512,128]{2,1,0:T(8,128)(2,1)S(1)}, u32[]{:S(2)}, u32[]{:S(2)}) collective-permute-start(bf16[2,512,128]{2,1,0:T(8,128)(2,1)} %get-tuple-element.41), channel_id=1, source_target_pairs={{0,4},{1,5},{2,6},{3,7},{4,0},{5,1},{6,2},{7,3},{8,12},{9,13},{10,... | collective-permute-start | bytes 786440 | tf_op jit(solution)/shard_map/ppermute | solution.py:371
  18.2 25.5 %collective-permute-start.13 = (bf16[2,512,128]{2,1,0:T(8,128)(2,1)}, bf16[2,512,128]{2,1,0:T(8,128)(2,1)S(1)}, u32[]{:S(2)}, u32[]{:S(2)}) collective-permute-start(bf16[2,512,128]{2,1,0:T(8,128)(2,1)} %get-tuple-element.42), channel_id=1, source_target_pairs={{0,5},{1,4},{2,7},{3,6},{4,1},{5,0},{6,3},{7,2},{8,13},{9,12},{10,... | collective-permute-start | bytes 786440 | tf_op jit(solution)/shard_map/ppermute | solution.py:371
  36.6 19.4 %copy-start.2 = (bf16[16,288,128]{2,1,0:T(8,128)(2,1)}, bf16[16,288,128]{2,1,0:T(8,128)(2,1)S(1)}, u32[]{:S(2)}) copy-start(bf16[16,288,128]{2,1,0:T(8,128)(2,1)S(1)} %all-to-all-done.refs_2_) | copy-start | bytes 3538948
  36.7 18.5 %collective-permute-start.7 = (bf16[2,512,128]{2,1,0:T(8,128)(2,1)}, bf16[2,512,128]{2,1,0:T(8,128)(2,1)S(1)}, u32[]{:S(2)}, u32[]{:S(2)}) collective-permute-start(bf16[2,512,128]{2,1,0:T(8,128)(2,1)} %get-tuple-element.35), channel_id=1, source_target_pairs={{0,6},{1,7},{2,4},{3,5},{4,2},{5,3},{6,0},{7,1},{8,14},{9,15},{10,... | collective-permute-start | bytes 786440 | tf_op jit(solution)/shard_map/ppermute | solution.py:371
  41.5 14.4 %collective-permute-start.8 = (bf16[2,512,128]{2,1,0:T(8,128)(2,1)}, bf16[2,512,128]{2,1,0:T(8,128)(2,1)S(1)}, u32[]{:S(2)}, u32[]{:S(2)}) collective-permute-start(bf16[2,512,128]{2,1,0:T(8,128)(2,1)} %get-tuple-element.36), channel_id=1, source_target_pairs={{0,7},{1,6},{2,5},{3,4},{4,3},{5,2},{6,1},{7,0},{8,15},{9,14},{10,... | collective-permute-start | bytes 786440 | tf_op jit(solution)/shard_map/ppermute | solution.py:371
  43.8 1.0 copy-start.8
  56.0 11.0 %copy-start = (bf16[2,512,8,128]{3,2,1,0:T(8,128)(2,1)S(1)}, bf16[2,512,8,128]{3,2,1,0:T(8,128)(2,1)}, u32[]{:S(2)}) copy-start(bf16[2,512,8,128]{3,2,1,0:T(8,128)(2,1)} %k_hbm.3) | copy-start | bytes 6291460
  62.9 42.8 %all-to-all-start.2 = ((bf16[16,136,128]{2,1,0:T(8,128)(2,1)}), bf16[16,136,128]{2,1,0:T(8,128)(2,1)S(1)}, u32[]{:S(2)}, u32[]{:S(2)}) async-start(bf16[16,136,128]{2,1,0:T(8,128)(2,1)} %copy-done.4), calls=%async_computation.2 | async-start | bytes 1114112 | tf_op jit(solution)/shard_map/all_to_all | solution.py:383
  67.0 1.6 %copy-start.1 = (bf16[2,512,8,128]{3,2,1,0:T(8,128)(2,1)S(1)}, bf16[2,512,8,128]{3,2,1,0:T(8,128)(2,1)}, u32[]{:S(2)}) copy-start(bf16[2,512,8,128]{3,2,1,0:T(8,128)(2,1)} %v_hbm.3) | copy-start | bytes 6291460
  68.6 21.1 %copy-start.3 = (bf16[16,288,128]{2,1,0:T(8,128)(2,1)S(1)}, bf16[16,288,128]{2,1,0:T(8,128)(2,1)}, u32[]{:S(2)}) copy-start(bf16[16,288,128]{2,1,0:T(8,128)(2,1)} %copy-done.2) | copy-start | bytes 3538948
  69.6 4.0 %collective-permute-start.2 = (bf16[2,512,128]{2,1,0:T(8,128)(2,1)S(1)}, bf16[2,512,128]{2,1,0:T(8,128)(2,1)S(1)}, u32[]{:S(2)}, u32[]{:S(2)}) collective-permute-start(bf16[2,512,128]{2,1,0:T(8,128)(2,1)S(1)} %get-tuple-element.28), channel_id=1, source_target_pairs={{0,1},{1,0},{2,3},{3,2},{4,5},{5,4},{6,7},{7,6},{8,9},{9,8},{10,11... | collective-permute-start | bytes 786440 | tf_op jit(solution)/shard_map/ppermute | solution.py:371
  70.1 12.1 %collective-permute-start.3 = (bf16[2,512,128]{2,1,0:T(8,128)(2,1)S(1)}, bf16[2,512,128]{2,1,0:T(8,128)(2,1)S(1)}, u32[]{:S(2)}, u32[]{:S(2)}) collective-permute-start(bf16[2,512,128]{2,1,0:T(8,128)(2,1)S(1)} %get-tuple-element.29), channel_id=1, source_target_pairs={{0,2},{1,3},{2,0},{3,1},{4,6},{5,7},{6,4},{7,5},{8,10},{9,11},{10,... | collective-permute-start | bytes 786440 | tf_op jit(solution)/shard_map/ppermute | solution.py:371
  71.7 15.3 %collective-permute-start.4 = (bf16[2,512,128]{2,1,0:T(8,128)(2,1)S(1)}, bf16[2,512,128]{2,1,0:T(8,128)(2,1)S(1)}, u32[]{:S(2)}, u32[]{:S(2)}) collective-permute-start(bf16[2,512,128]{2,1,0:T(8,128)(2,1)S(1)} %get-tuple-element.30), channel_id=1, source_target_pairs={{0,3},{1,2},{2,1},{3,0},{4,7},{5,6},{6,5},{7,4},{8,11},{9,10},{10,... | collective-permute-start | bytes 786440 | tf_op jit(solution)/shard_map/ppermute | solution.py:371
  71.7 15.3 %collective-permute-start.5 = (bf16[2,512,128]{2,1,0:T(8,128)(2,1)S(1)}, bf16[2,512,128]{2,1,0:T(8,128)(2,1)S(1)}, u32[]{:S(2)}, u32[]{:S(2)}) collective-permute-start(bf16[2,512,128]{2,1,0:T(8,128)(2,1)S(1)} %get-tuple-element.31), channel_id=1, source_target_pairs={{0,4},{1,5},{2,6},{3,7},{4,0},{5,1},{6,2},{7,3},{8,12},{9,13},{10,... | collective-permute-start | bytes 786440 | tf_op jit(solution)/shard_map/ppermute | solution.py:371
  73.5 16.2 %collective-permute-start.6 = (bf16[2,512,128]{2,1,0:T(8,128)(2,1)S(1)}, bf16[2,512,128]{2,1,0:T(8,128)(2,1)S(1)}, u32[]{:S(2)}, u32[]{:S(2)}) collective-permute-start(bf16[2,512,128]{2,1,0:T(8,128)(2,1)S(1)} %get-tuple-element.32), channel_id=1, source_target_pairs={{0,5},{1,4},{2,7},{3,6},{4,1},{5,0},{6,3},{7,2},{8,13},{9,12},{10,... | collective-permute-start | bytes 786440 | tf_op jit(solution)/shard_map/ppermute | solution.py:371
  73.6 26.5 %collective-permute-start = (bf16[2,512,128]{2,1,0:T(8,128)(2,1)S(1)}, bf16[2,512,128]{2,1,0:T(8,128)(2,1)S(1)}, u32[]{:S(2)}, u32[]{:S(2)}) collective-permute-start(bf16[2,512,128]{2,1,0:T(8,128)(2,1)S(1)} %get-tuple-element.25), channel_id=1, source_target_pairs={{0,6},{1,7},{2,4},{3,5},{4,2},{5,3},{6,0},{7,1},{8,14},{9,15},{10,... | collective-permute-start | bytes 786440 | tf_op jit(solution)/shard_map/ppermute | solution.py:371
  82.2 20.1 %collective-permute-start.1 = (bf16[2,512,128]{2,1,0:T(8,128)(2,1)S(1)}, bf16[2,512,128]{2,1,0:T(8,128)(2,1)S(1)}, u32[]{:S(2)}, u32[]{:S(2)}) collective-permute-start(bf16[2,512,128]{2,1,0:T(8,128)(2,1)S(1)} %get-tuple-element.26), channel_id=1, source_target_pairs={{0,7},{1,6},{2,5},{3,4},{4,3},{5,2},{6,1},{7,0},{8,15},{9,14},{10,... | collective-permute-start | bytes 786440 | tf_op jit(solution)/shard_map/ppermute | solution.py:371
  105.7 20.0 %all-to-all-start.1 = ((bf16[16,136,128]{2,1,0:T(8,128)(2,1)}), bf16[16,136,128]{2,1,0:T(8,128)(2,1)S(1)}, u32[]{:S(2)}, u32[]{:S(2)}) async-start(bf16[16,136,128]{2,1,0:T(8,128)(2,1)} %shard_map.67), calls=%async_computation.1 | async-start | bytes 1114112 | tf_op jit(solution)/shard_map/all_to_all | solution.py:383
  (3 other events, 2.3 us)
where the time goes:
time: 129 us; the launch traced here: 127 us
  waiting for transfers between devices  48.1 us (37%)
  Pallas kernels  38.3 us (30%)
  starting transfers between devices  33.7 us (26%)
  local copies, waits for them, and re-layouts  6.6 us (5%)
    pallas_call x4, Pallas kernels, attend(): pl.pallas_call(functools.partial(attend_kernel, order=order, blocks=len(k...  30.3 us
    all_to_all x1, waiting for transfers between devices, attention(): lax.all_to_all(pack(queries, new_k, new_v, devices_seq), 'seq', split_axi...  17.5 us
    ppermute x14, starting transfers between devices, attention(): lax.ppermute(parts[k], 'seq', [(i, i ^ k) for i in range(devices_seq)])  17.1 us
    ppermute x14, waiting for transfers between devices, attention(): lax.ppermute(parts[k], 'seq', [(i, i ^ k) for i in range(devices_seq)])  17 us
    all_to_all x2, waiting for transfers between devices, attention(): part = lax.all_to_all(part, 'seq', split_axis=0, concat_axis=0, tiled=True)  13.5 us
    all_to_all x2, starting transfers between devices, attention(): part = lax.all_to_all(part, 'seq', split_axis=0, concat_axis=0, tiled=True)  9.26 us
    all_to_all x1, starting transfers between devices, attention(): lax.all_to_all(pack(queries, new_k, new_v, devices_seq), 'seq', split_axi...  7.39 us
    unnamed x20, local copies, waits for them, and re-layouts  5.92 us
  transfers between devices with their start and end apart: 17, of which 8 were waited for; matrix products, arithmetic and copies ran while one was open for 1% of the time, Pallas kernels for 23%

commit v1 on v0

--- a/solution.py
+++ b/solution.py
@@ -377,9 +377,8 @@
         rows = (r * per_source, per_source, group_size)
         common = (cache_len[r : r + 1], place, head_q, kv_blocks[r])
         fresh_r = (head_fresh[0, r], head_fresh[1, r])
-        first = kv_heads - 2
-        state = attend(*common, tuple(range(first)), fresh_r, None, False, *rows)
-        part = attend(*common, tuple(range(first, kv_heads)), None, state, True, *rows)
+        state, first = None, 0
+        part = attend(*common, tuple(range(first, kv_heads)), fresh_r, state, True, *rows)
         part = lax.all_to_all(part, "seq", split_axis=0, concat_axis=0, tiled=True)
         part = part.reshape(spread, kv_heads, per_source + STAT_ROWS, head_dim)
         out = merge(part, r, requests, local_rows, group_size, out)

time: 129 us -> 152 us (1.18)
  waiting for transfers between devices: 48.1 us -> 69.6 us
  local copies, waits for them, and re-layouts: 6.6 us -> 16.7 us
  starting transfers between devices: 33.7 us -> 29 us
  Pallas kernels: 38.3 us -> 34.1 us
    ppermute x14, waiting for transfers between devices: 17 us -> 50 us  [attention(): lax.ppermute(parts[k], 'seq', [(i, i ^ k) for i in range(devices_seq)])]
    all_to_all x1, waiting for transfers between devices: 17.5 us -> 6.05 us  [attention(): lax.all_to_all(pack(queries, new_k, new_v, devices_seq), 'seq', split_axi...]
    unnamed x20 -> x48, local copies, waits for them, and re-layouts: 5.92 us -> 16.1 us
    pallas_call x4 -> x2, Pallas kernels: 30.3 us -> 26.1 us  [attend(): pl.pallas_call(functools.partial(attend_kernel, order=order, blocks=len(k...]
    ppermute x14, starting transfers between devices: 17.1 us -> 14.5 us  [attention(): lax.ppermute(parts[k], 'seq', [(i, i ^ k) for i in range(devices_seq)])]
    all_to_all x2, starting transfers between devices: 9.26 us -> 7.17 us  [attention(): part = lax.all_to_all(part, 'seq', split_axis=0, concat_axis=0, tiled=True)]
  transfers between devices with their start and end apart: 17 -> 17, of which waited for: 8 -> 13; matrix products, arithmetic and copies ran while one was open for 1% -> 0% of each run, Pallas kernels for 23% -> 12%
where the time goes in v1:
time: 152 us; the launch traced here: 150 us
  waiting for transfers between devices  69.6 us (46%)
  Pallas kernels  34.1 us (22%)
  starting transfers between devices  29 us (19%)
  local copies, waits for them, and re-layouts  16.7 us (11%)
    ppermute x14, waiting for transfers between devices, attention(): lax.ppermute(parts[k], 'seq', [(i, i ^ k) for i in range(devices_seq)])  50 us
    pallas_call x2, Pallas kernels, attend(): pl.pallas_call(functools.partial(attend_kernel, order=order, blocks=len(k...  26.1 us
    unnamed x48, local copies, waits for them, and re-layouts  16.1 us
    ppermute x14, starting transfers between devices, attention(): lax.ppermute(parts[k], 'seq', [(i, i ^ k) for i in range(devices_seq)])  14.5 us
    all_to_all x2, waiting for transfers between devices, attention(): part = lax.all_to_all(part, 'seq', split_axis=0, concat_axis=0, tiled=True)  13.5 us
    all_to_all x1, starting transfers between devices, attention(): lax.all_to_all(pack(queries, new_k, new_v, devices_seq), 'seq', split_axi...  7.39 us
    all_to_all x2, starting transfers between devices, attention(): part = lax.all_to_all(part, 'seq', split_axis=0, concat_axis=0, tiled=True)  7.17 us
    all_to_all x1, waiting for transfers between devices, attention(): lax.all_to_all(pack(queries, new_k, new_v, devices_seq), 'seq', split_axi...  6.05 us
  transfers between devices with their start and end apart: 17, of which 13 were waited for; matrix products, arithmetic and copies ran while one was open for 0% of the time, Pallas kernels for 12%

profile of v1, /device:TPU:0, one launch (start us, length us, event | category | flops | bytes accessed | tf_op | source)
XLA Modules:
  0.0 149.7 jit_solution(4792379612419283464)
XLA Ops:
  3.7 7.4 %all-to-all-start = ((bf16[16,288,128]{2,1,0:T(8,128)(2,1)}), bf16[16,288,128]{2,1,0:T(8,128)(2,1)S(1)}, u32[]{:S(2)}, u32[]{:S(2)}) async-start(bf16[16,288,128]{2,1,0:T(8,128)(2,1)} %shard_map.64), calls=%async_computation | async-start | bytes 2359296 | tf_op jit(solution)/shard_map/all_to_all | solution.py:358
  11.1 3.3 %shard_map.67 = (bf16[2,512,128]{2,1,0:T(8,128)(2,1)}, bf16[2,512,128]{2,1,0:T(8,128)(2,1)}, bf16[2,512,128]{2,1,0:T(8,128)(2,1)}, bf16[2,512,128]{2,1,0:T(8,128...) custom-call(s32[1]{0:T(128)} %bitcast.own_ref, ...), custom_call_target="tpu_custom_call" | custom-call | tf_op jit(solution)/shard_map/pallas_call | solution.py:333
  14.9 1.6 %collective-permute-start.8 = (bf16[2,512,128]{2,1,0:T(8,128)(2,1)}, bf16[2,512,128]{2,1,0:T(8,128)(2,1)S(1)}, u32[]{:S(2)}, u32[]{:S(2)}) collective-permute-start(bf16[2,512,128]{2,1,0:T(8,128)(2,1)} %get-tuple-element.31), channel_id=1, source_target_pairs={{0,2},{1,3},{2,0},{3,1},{4,6},{5,7},{6,4},{7,5},{8,10},{9,11},{10,... | collective-permute-start | bytes 786440 | tf_op jit(solution)/shard_map/ppermute | solution.py:371
  16.5 1.7 %collective-permute-start.10 = (bf16[2,512,128]{2,1,0:T(8,128)(2,1)}, bf16[2,512,128]{2,1,0:T(8,128)(2,1)S(1)}, u32[]{:S(2)}, u32[]{:S(2)}) collective-permute-start(bf16[2,512,128]{2,1,0:T(8,128)(2,1)} %get-tuple-element.33), channel_id=1, source_target_pairs={{0,4},{1,5},{2,6},{3,7},{4,0},{5,1},{6,2},{7,3},{8,12},{9,13},{10,... | collective-permute-start | bytes 786440 | tf_op jit(solution)/shard_map/ppermute | solution.py:371
  19.0 2.5 %collective-permute-start.12 = (bf16[2,512,128]{2,1,0:T(8,128)(2,1)}, bf16[2,512,128]{2,1,0:T(8,128)(2,1)S(1)}, u32[]{:S(2)}, u32[]{:S(2)}) collective-permute-start(bf16[2,512,128]{2,1,0:T(8,128)(2,1)} %get-tuple-element.35), channel_id=1, source_target_pairs={{0,6},{1,7},{2,4},{3,5},{4,2},{5,3},{6,0},{7,1},{8,14},{9,15},{10,... | collective-permute-start | bytes 786440 | tf_op jit(solution)/shard_map/ppermute | solution.py:371
  21.5 9.0 %collective-permute-done.8.refs_5_ = bf16[2,512,128]{2,1,0:T(8,128)(2,1)S(1)} collective-permute-done((bf16[2,512,128]{2,1,0:T(8,128)(2,1)}, bf16[2,512,128]{2,1,0:T(8,128)(2,1)S(1)}, u32[]{:S(2)}, u32[]{:S(2)}) %collective-permute-start.8) | collective-permute-done | bytes 262176 | tf_op jit(solution)/shard_map/ppermute | solution.py:371
  30.6 6.1 %all-to-all-done.refs_2_ = bf16[16,288,128]{2,1,0:T(8,128)(2,1)S(1)} async-done(((bf16[16,288,128]{2,1,0:T(8,128)(2,1)}), bf16[16,288,128]{2,1,0:T(8,128)(2,1)S(1)}, u32[]{:S(2)}, u32[]{:S(2)}) %all-to-all-start) | async-done | bytes 1179680 | tf_op jit(solution)/shard_map/all_to_all | solution.py:358
  40.0 3.8 %collective-permute-done.11.refs_8_ = bf16[2,512,128]{2,1,0:T(8,128)(2,1)S(1)} collective-permute-done((bf16[2,512,128]{2,1,0:T(8,128)(2,1)}, bf16[2,512,128]{2,1,0:T(8,128)(2,1)S(1)}, u32[]{:S(2)}, u32[]{:S(2)}) %collective-permute-start.11) | collective-permute-done | bytes 262176 | tf_op jit(solution)/shard_map/ppermute | solution.py:371
  44.5 7.0 %collective-permute-done.12.refs_9_ = bf16[2,512,128]{2,1,0:T(8,128)(2,1)S(1)} collective-permute-done((bf16[2,512,128]{2,1,0:T(8,128)(2,1)}, bf16[2,512,128]{2,1,0:T(8,128)(2,1)S(1)}, u32[]{:S(2)}, u32[]{:S(2)}) %collective-permute-start.12) | collective-permute-done | bytes 262176 | tf_op jit(solution)/shard_map/ppermute | solution.py:371
  52.2 3.8 %collective-permute-done.13.refs_10_ = bf16[2,512,128]{2,1,0:T(8,128)(2,1)S(1)} collective-permute-done((bf16[2,512,128]{2,1,0:T(8,128)(2,1)}, bf16[2,512,128]{2,1,0:T(8,128)(2,1)S(1)}, u32[]{:S(2)}, u32[]{:S(2)}) %collective-permute-start.13) | collective-permute-done | bytes 262176 | tf_op jit(solution)/shard_map/ppermute | solution.py:371
  64.3 13.7 %shard_map.68 = bf16[16,136,128]{2,1,0:T(8,128)(2,1)S(1)} custom-call(s32[1]{0:T(128)} %get-tuple-element.41.refs_0_, s32[2]{0:T(128)S(1)} %pad_add_fusion.refs_1_, bf16[16,288,128]{2,1,0:T(8,128)(2,1)S(1)} %all-to-all-done.refs_2_, bf16[2,512,128]{2,1,0:T(8,128)(2,1)S(1)} %copy-done.8, bf16[2,512,128]{2,1,0:T(8,128)(2,1)S(1)} %copy-done.10, ...), custom_call_target="tpu_custom_call" | custom-call | flops 4294967296 | bytes 3145728 | tf_op jit(solution)/shard_map/pallas_call | solution.py:224
  78.9 3.6 %all-to-all-start.2 = ((bf16[16,136,128]{2,1,0:T(8,128)(2,1)}), bf16[16,136,128]{2,1,0:T(8,128)(2,1)S(1)}, u32[]{:S(2)}, u32[]{:S(2)}) async-start(bf16[16,136,128]{2,1,0:T(8,128)(2,1)} %copy-done.4), calls=%async_computation.2 | async-start | bytes 1114112 | tf_op jit(solution)/shard_map/all_to_all | solution.py:382
  82.5 1.6 %copy-done.1 = bf16[2,512,8,128]{3,2,1,0:T(8,128)(2,1)S(1)} copy-done((bf16[2,512,8,128]{3,2,1,0:T(8,128)(2,1)S(1)}, bf16[2,512,8,128]{3,2,1,0:T(8,128)(2,1)}, u32[]{:S(2)}) %copy-start.1) | copy-done | bytes 2097176
  85.4 1.6 %collective-permute-start.1 = (bf16[2,512,128]{2,1,0:T(8,128)(2,1)S(1)}, bf16[2,512,128]{2,1,0:T(8,128)(2,1)S(1)}, u32[]{:S(2)}, u32[]{:S(2)}) collective-permute-start(bf16[2,512,128]{2,1,0:T(8,128)(2,1)S(1)} %get-tuple-element.23), channel_id=1, source_target_pairs={{0,2},{1,3},{2,0},{3,1},{4,6},{5,7},{6,4},{7,5},{8,10},{9,11},{10,... | collective-permute-start | bytes 786440 | tf_op jit(solution)/shard_map/ppermute | solution.py:371
  87.1 1.7 %collective-permute-start.3 = (bf16[2,512,128]{2,1,0:T(8,128)(2,1)S(1)}, bf16[2,512,128]{2,1,0:T(8,128)(2,1)S(1)}, u32[]{:S(2)}, u32[]{:S(2)}) collective-permute-start(bf16[2,512,128]{2,1,0:T(8,128)(2,1)S(1)} %get-tuple-element.25), channel_id=1, source_target_pairs={{0,4},{1,5},{2,6},{3,7},{4,0},{5,1},{6,2},{7,3},{8,12},{9,13},{10,... | collective-permute-start | bytes 786440 | tf_op jit(solution)/shard_map/ppermute | solution.py:371
  88.9 2.6 %collective-permute-start.5 = (bf16[2,512,128]{2,1,0:T(8,128)(2,1)S(1)}, bf16[2,512,128]{2,1,0:T(8,128)(2,1)S(1)}, u32[]{:S(2)}, u32[]{:S(2)}) collective-permute-start(bf16[2,512,128]{2,1,0:T(8,128)(2,1)S(1)} %get-tuple-element.27), channel_id=1, source_target_pairs={{0,6},{1,7},{2,4},{3,5},{4,2},{5,3},{6,0},{7,1},{8,14},{9,15},{10,... | collective-permute-start | bytes 786440 | tf_op jit(solution)/shard_map/ppermute | solution.py:371
  91.5 6.0 %collective-permute-done.1.refs_5_ = bf16[2,512,128]{2,1,0:T(8,128)(2,1)S(1)} collective-permute-done((bf16[2,512,128]{2,1,0:T(8,128)(2,1)S(1)}, bf16[2,512,128]{2,1,0:T(8,128)(2,1)S(1)}, u32[]{:S(2)}, u32[]{:S(2)}) %collective-permute-start.1) | collective-permute-done | bytes 262176 | tf_op jit(solution)/shard_map/ppermute | solution.py:371
  99.0 3.4 %collective-permute-done.2.refs_6_ = bf16[2,512,128]{2,1,0:T(8,128)(2,1)S(1)} collective-permute-done((bf16[2,512,128]{2,1,0:T(8,128)(2,1)S(1)}, bf16[2,512,128]{2,1,0:T(8,128)(2,1)S(1)}, u32[]{:S(2)}, u32[]{:S(2)}) %collective-permute-start.2) | collective-permute-done | bytes 262176 | tf_op jit(solution)/shard_map/ppermute | solution.py:371
  102.4 2.7 %collective-permute-done.4.refs_8_ = bf16[2,512,128]{2,1,0:T(8,128)(2,1)S(1)} collective-permute-done((bf16[2,512,128]{2,1,0:T(8,128)(2,1)S(1)}, bf16[2,512,128]{2,1,0:T(8,128)(2,1)S(1)}, u32[]{:S(2)}, u32[]{:S(2)}) %collective-permute-start.4) | collective-permute-done | bytes 262176 | tf_op jit(solution)/shard_map/ppermute | solution.py:371
  105.1 7.3 %collective-permute-done.5.refs_9_ = bf16[2,512,128]{2,1,0:T(8,128)(2,1)S(1)} collective-permute-done((bf16[2,512,128]{2,1,0:T(8,128)(2,1)S(1)}, bf16[2,512,128]{2,1,0:T(8,128)(2,1)S(1)}, u32[]{:S(2)}, u32[]{:S(2)}) %collective-permute-start.5) | collective-permute-done | bytes 262176 | tf_op jit(solution)/shard_map/ppermute | solution.py:371
  112.3 5.3 %collective-permute-done.6.refs_10_ = bf16[2,512,128]{2,1,0:T(8,128)(2,1)S(1)} collective-permute-done((bf16[2,512,128]{2,1,0:T(8,128)(2,1)S(1)}, bf16[2,512,128]{2,1,0:T(8,128)(2,1)S(1)}, u32[]{:S(2)}, u32[]{:S(2)}) %collective-permute-start.6) | collective-permute-done | bytes 262176 | tf_op jit(solution)/shard_map/ppermute | solution.py:371
  117.6 12.4 %shard_map.66 = bf16[16,136,128]{2,1,0:T(8,128)(2,1)} custom-call(s32[1]{0:T(128)} %get-tuple-element.42.refs_0_, s32[2]{0:T(128)S(1)} %pad_add_fusion.refs_1_, bf16[16,288,128]{2,1,0:T(8,128)(2,1)S(1)} %copy-done.3, bf16[2,512,128]{2,1,0:T(8,128)(2,1)S(1)} %get-tuple-element.21.refs_3_, bf16[2,512,128]{2,1,0:T(8,128)(2,1)S(1)} %collective-permute-done.refs_4_, ...), custom_call_target="tpu_custom_call" | custom-call | flops 4294967296 | bytes 3145728 | tf_op jit(solution)/shard_map/pallas_call | solution.py:224
  130.0 3.6 %all-to-all-start.1 = ((bf16[16,136,128]{2,1,0:T(8,128)(2,1)}), bf16[16,136,128]{2,1,0:T(8,128)(2,1)S(1)}, u32[]{:S(2)}, u32[]{:S(2)}) async-start(bf16[16,136,128]{2,1,0:T(8,128)(2,1)} %shard_map.66), calls=%async_computation.1 | async-start | bytes 1114112 | tf_op jit(solution)/shard_map/all_to_all | solution.py:382
  134.9 13.5 %all-to-all-done.1 = bf16[16,136,128]{2,1,0:T(8,128)(2,1)S(1)} async-done(((bf16[16,136,128]{2,1,0:T(8,128)(2,1)}), bf16[16,136,128]{2,1,0:T(8,128)(2,1)S(1)}, u32[]{:S(2)}, u32[]{:S(2)}) %all-to-all-start.1) | async-done | bytes 557088 | tf_op jit(solution)/shard_map/all_to_all | solution.py:382
  (70 shorter events, 24.5 us)
Async XLA Ops:
  3.7 32.9 %all-to-all-start = ((bf16[16,288,128]{2,1,0:T(8,128)(2,1)}), bf16[16,288,128]{2,1,0:T(8,128)(2,1)S(1)}, u32[]{:S(2)}, u32[]{:S(2)}) async-start(bf16[16,288,128]{2,1,0:T(8,128)(2,1)} %shard_map.64), calls=%async_computation | async-start | bytes 2359296 | tf_op jit(solution)/shard_map/all_to_all | solution.py:358
  11.1 7.3 %copy-start.23 = (s32[2]{0:T(128)S(1)}, s32[2]{0:T(128)}, u32[]{:S(2)}) copy-start(s32[2]{0:T(128)} %param.11) | copy-start | bytes 28
  14.4 4.6 %collective-permute-start.7 = (bf16[2,512,128]{2,1,0:T(8,128)(2,1)}, bf16[2,512,128]{2,1,0:T(8,128)(2,1)S(1)}, u32[]{:S(2)}, u32[]{:S(2)}) collective-permute-start(bf16[2,512,128]{2,1,0:T(8,128)(2,1)} %get-tuple-element.30), channel_id=1, source_target_pairs={{0,1},{1,0},{2,3},{3,2},{4,5},{5,4},{6,7},{7,6},{8,9},{9,8},{10,11... | collective-permute-start | bytes 786440 | tf_op jit(solution)/shard_map/ppermute | solution.py:371
  14.9 15.6 %collective-permute-start.8 = (bf16[2,512,128]{2,1,0:T(8,128)(2,1)}, bf16[2,512,128]{2,1,0:T(8,128)(2,1)S(1)}, u32[]{:S(2)}, u32[]{:S(2)}) collective-permute-start(bf16[2,512,128]{2,1,0:T(8,128)(2,1)} %get-tuple-element.31), channel_id=1, source_target_pairs={{0,2},{1,3},{2,0},{3,1},{4,6},{5,7},{6,4},{7,5},{8,10},{9,11},{10,... | collective-permute-start | bytes 786440 | tf_op jit(solution)/shard_map/ppermute | solution.py:371
  16.5 21.1 %collective-permute-start.9 = (bf16[2,512,128]{2,1,0:T(8,128)(2,1)}, bf16[2,512,128]{2,1,0:T(8,128)(2,1)S(1)}, u32[]{:S(2)}, u32[]{:S(2)}) collective-permute-start(bf16[2,512,128]{2,1,0:T(8,128)(2,1)} %get-tuple-element.32), channel_id=1, source_target_pairs={{0,3},{1,2},{2,1},{3,0},{4,7},{5,6},{6,5},{7,4},{8,11},{9,10},{10,... | collective-permute-start | bytes 786440 | tf_op jit(solution)/shard_map/ppermute | solution.py:371
  16.5 22.8 %collective-permute-start.10 = (bf16[2,512,128]{2,1,0:T(8,128)(2,1)}, bf16[2,512,128]{2,1,0:T(8,128)(2,1)S(1)}, u32[]{:S(2)}, u32[]{:S(2)}) collective-permute-start(bf16[2,512,128]{2,1,0:T(8,128)(2,1)} %get-tuple-element.33), channel_id=1, source_target_pairs={{0,4},{1,5},{2,6},{3,7},{4,0},{5,1},{6,2},{7,3},{8,12},{9,13},{10,... | collective-permute-start | bytes 786440 | tf_op jit(solution)/shard_map/ppermute | solution.py:371
  18.2 25.6 %collective-permute-start.11 = (bf16[2,512,128]{2,1,0:T(8,128)(2,1)}, bf16[2,512,128]{2,1,0:T(8,128)(2,1)S(1)}, u32[]{:S(2)}, u32[]{:S(2)}) collective-permute-start(bf16[2,512,128]{2,1,0:T(8,128)(2,1)} %get-tuple-element.34), channel_id=1, source_target_pairs={{0,5},{1,4},{2,7},{3,6},{4,1},{5,0},{6,3},{7,2},{8,13},{9,12},{10,... | collective-permute-start | bytes 786440 | tf_op jit(solution)/shard_map/ppermute | solution.py:371
  19.0 37.7 %copy-start.9 = (bf16[2,512,128]{2,1,0:T(8,128)(2,1)}, bf16[2,512,128]{2,1,0:T(8,128)(2,1)S(1)}, u32[]{:S(2)}) copy-start(bf16[2,512,128]{2,1,0:T(8,128)(2,1)S(1)} %collective-permute-done.7.refs_4_) | copy-start | bytes 786436
  19.0 32.6 %collective-permute-start.12 = (bf16[2,512,128]{2,1,0:T(8,128)(2,1)}, bf16[2,512,128]{2,1,0:T(8,128)(2,1)S(1)}, u32[]{:S(2)}, u32[]{:S(2)}) collective-permute-start(bf16[2,512,128]{2,1,0:T(8,128)(2,1)} %get-tuple-element.35), channel_id=1, source_target_pairs={{0,6},{1,7},{2,4},{3,5},{4,2},{5,3},{6,0},{7,1},{8,14},{9,15},{10,... | collective-permute-start | bytes 786440 | tf_op jit(solution)/shard_map/ppermute | solution.py:371
  30.5 26.2 %copy-start.11 = (bf16[2,512,128]{2,1,0:T(8,128)(2,1)}, bf16[2,512,128]{2,1,0:T(8,128)(2,1)S(1)}, u32[]{:S(2)}) copy-start(bf16[2,512,128]{2,1,0:T(8,128)(2,1)S(1)} %collective-permute-done.8.refs_5_) | copy-start | bytes 786436
  30.5 25.5 %collective-permute-start.13 = (bf16[2,512,128]{2,1,0:T(8,128)(2,1)}, bf16[2,512,128]{2,1,0:T(8,128)(2,1)S(1)}, u32[]{:S(2)}, u32[]{:S(2)}) collective-permute-start(bf16[2,512,128]{2,1,0:T(8,128)(2,1)} %get-tuple-element.36), channel_id=1, source_target_pairs={{0,7},{1,6},{2,5},{3,4},{4,3},{5,2},{6,1},{7,0},{8,15},{9,14},{10,... | collective-permute-start | bytes 786440 | tf_op jit(solution)/shard_map/ppermute | solution.py:371
  36.6 41.4 %copy-start.2 = (bf16[16,288,128]{2,1,0:T(8,128)(2,1)}, bf16[16,288,128]{2,1,0:T(8,128)(2,1)S(1)}, u32[]{:S(2)}) copy-start(bf16[16,288,128]{2,1,0:T(8,128)(2,1)S(1)} %all-to-all-done.refs_2_) | copy-start | bytes 3538948
  64.3 18.1 %copy-start = (bf16[2,512,8,128]{3,2,1,0:T(8,128)(2,1)S(1)}, bf16[2,512,8,128]{3,2,1,0:T(8,128)(2,1)}, u32[]{:S(2)}) copy-start(bf16[2,512,8,128]{3,2,1,0:T(8,128)(2,1)} %k_hbm.3) | copy-start | bytes 6291460
  78.9 51.2 %all-to-all-start.2 = ((bf16[16,136,128]{2,1,0:T(8,128)(2,1)}), bf16[16,136,128]{2,1,0:T(8,128)(2,1)S(1)}, u32[]{:S(2)}, u32[]{:S(2)}) async-start(bf16[16,136,128]{2,1,0:T(8,128)(2,1)} %copy-done.4), calls=%async_computation.2 | async-start | bytes 1114112 | tf_op jit(solution)/shard_map/all_to_all | solution.py:382
  82.4 1.6 %copy-start.1 = (bf16[2,512,8,128]{3,2,1,0:T(8,128)(2,1)S(1)}, bf16[2,512,8,128]{3,2,1,0:T(8,128)(2,1)}, u32[]{:S(2)}) copy-start(bf16[2,512,8,128]{3,2,1,0:T(8,128)(2,1)} %v_hbm.3) | copy-start | bytes 6291460
  84.0 33.6 %copy-start.3 = (bf16[16,288,128]{2,1,0:T(8,128)(2,1)S(1)}, bf16[16,288,128]{2,1,0:T(8,128)(2,1)}, u32[]{:S(2)}) copy-start(bf16[16,288,128]{2,1,0:T(8,128)(2,1)} %copy-done.2) | copy-start | bytes 3538948
  85.1 3.9 %collective-permute-start = (bf16[2,512,128]{2,1,0:T(8,128)(2,1)S(1)}, bf16[2,512,128]{2,1,0:T(8,128)(2,1)S(1)}, u32[]{:S(2)}, u32[]{:S(2)}) collective-permute-start(bf16[2,512,128]{2,1,0:T(8,128)(2,1)S(1)} %get-tuple-element.22), channel_id=1, source_target_pairs={{0,1},{1,0},{2,3},{3,2},{4,5},{5,4},{6,7},{7,6},{8,9},{9,8},{10,11... | collective-permute-start | bytes 786440 | tf_op jit(solution)/shard_map/ppermute | solution.py:371
  85.4 12.0 %collective-permute-start.1 = (bf16[2,512,128]{2,1,0:T(8,128)(2,1)S(1)}, bf16[2,512,128]{2,1,0:T(8,128)(2,1)S(1)}, u32[]{:S(2)}, u32[]{:S(2)}) collective-permute-start(bf16[2,512,128]{2,1,0:T(8,128)(2,1)S(1)} %get-tuple-element.23), channel_id=1, source_target_pairs={{0,2},{1,3},{2,0},{3,1},{4,6},{5,7},{6,4},{7,5},{8,10},{9,11},{10,... | collective-permute-start | bytes 786440 | tf_op jit(solution)/shard_map/ppermute | solution.py:371
  87.1 15.3 %collective-permute-start.2 = (bf16[2,512,128]{2,1,0:T(8,128)(2,1)S(1)}, bf16[2,512,128]{2,1,0:T(8,128)(2,1)S(1)}, u32[]{:S(2)}, u32[]{:S(2)}) collective-permute-start(bf16[2,512,128]{2,1,0:T(8,128)(2,1)S(1)} %get-tuple-element.24), channel_id=1, source_target_pairs={{0,3},{1,2},{2,1},{3,0},{4,7},{5,6},{6,5},{7,4},{8,11},{9,10},{10,... | collective-permute-start | bytes 786440 | tf_op jit(solution)/shard_map/ppermute | solution.py:371
  87.1 15.3 %collective-permute-start.3 = (bf16[2,512,128]{2,1,0:T(8,128)(2,1)S(1)}, bf16[2,512,128]{2,1,0:T(8,128)(2,1)S(1)}, u32[]{:S(2)}, u32[]{:S(2)}) collective-permute-start(bf16[2,512,128]{2,1,0:T(8,128)(2,1)S(1)} %get-tuple-element.25), channel_id=1, source_target_pairs={{0,4},{1,5},{2,6},{3,7},{4,0},{5,1},{6,2},{7,3},{8,12},{9,13},{10,... | collective-permute-start | bytes 786440 | tf_op jit(solution)/shard_map/ppermute | solution.py:371
  88.8 16.2 %collective-permute-start.4 = (bf16[2,512,128]{2,1,0:T(8,128)(2,1)S(1)}, bf16[2,512,128]{2,1,0:T(8,128)(2,1)S(1)}, u32[]{:S(2)}, u32[]{:S(2)}) collective-permute-start(bf16[2,512,128]{2,1,0:T(8,128)(2,1)S(1)} %get-tuple-element.26), channel_id=1, source_target_pairs={{0,5},{1,4},{2,7},{3,6},{4,1},{5,0},{6,3},{7,2},{8,13},{9,12},{10,... | collective-permute-start | bytes 786440 | tf_op jit(solution)/shard_map/ppermute | solution.py:371
  88.9 23.4 %collective-permute-start.5 = (bf16[2,512,128]{2,1,0:T(8,128)(2,1)S(1)}, bf16[2,512,128]{2,1,0:T(8,128)(2,1)S(1)}, u32[]{:S(2)}, u32[]{:S(2)}) collective-permute-start(bf16[2,512,128]{2,1,0:T(8,128)(2,1)S(1)} %get-tuple-element.27), channel_id=1, source_target_pairs={{0,6},{1,7},{2,4},{3,5},{4,2},{5,3},{6,0},{7,1},{8,14},{9,15},{10,... | collective-permute-start | bytes 786440 | tf_op jit(solution)/shard_map/ppermute | solution.py:371
  97.4 20.2 %collective-permute-start.6 = (bf16[2,512,128]{2,1,0:T(8,128)(2,1)S(1)}, bf16[2,512,128]{2,1,0:T(8,128)(2,1)S(1)}, u32[]{:S(2)}, u32[]{:S(2)}) collective-permute-start(bf16[2,512,128]{2,1,0:T(8,128)(2,1)S(1)} %get-tuple-element.28), channel_id=1, source_target_pairs={{0,7},{1,6},{2,5},{3,4},{4,3},{5,2},{6,1},{7,0},{8,15},{9,14},{10,... | collective-permute-start | bytes 786440 | tf_op jit(solution)/shard_map/ppermute | solution.py:371
  130.0 18.4 %all-to-all-start.1 = ((bf16[16,136,128]{2,1,0:T(8,128)(2,1)}), bf16[16,136,128]{2,1,0:T(8,128)(2,1)S(1)}, u32[]{:S(2)}, u32[]{:S(2)}) async-start(bf16[16,136,128]{2,1,0:T(8,128)(2,1)} %shard_map.66), calls=%async_computation.1 | async-start | bytes 1114112 | tf_op jit(solution)/shard_map/all_to_all | solution.py:382
  (17 other events, 14.5 us)
